TPU v7x, 32 devices: a whole 2x2x4 slice. The times are simulated.
32 devices in a mesh: rep: 4 (over x, core), shard: 4 (over z), ctx: 2 (over y).
Axes of the slice: x: 2, y: 2, z: 4, core: 2. Of those that a mesh axis runs over, the one named last changes fastest.
Arguments:
- block_input: bfloat16 [16, 256, 768], P(('rep', 'shard'), 'ctx'), may hold values from -6 to 6
- cotangent: bfloat16 [16, 256, 768], P(('rep', 'shard'), 'ctx'), may hold values from -6 to 6
- attend: float32 [2, 768, 2304], P(None, ('shard', 'ctx')), may hold values from -4 to 4
- project: float32 [2, 768, 768], P(None, ('shard', 'ctx')), may hold values from -1.25 to 1.25
- expand: float32 [2, 768, 3072], P(None, ('shard', 'ctx')), may hold values from -0.21875 to 0.21875
- contract: float32 [2, 3072, 768], P(None, ('shard', 'ctx')), may hold values from -0.109375 to 0.109375
- gains: float32 [2, 2, 768], P(None, None, ('shard', 'ctx')), may hold values from 0.5 to 1.5
- biases: float32 [2, 11, 768], P(None, None, ('shard', 'ctx')), may hold values from -3 to 3
- attend_drift: float32 [2, 768, 2304], P(None, ('shard', 'ctx')), may hold values from -112 to 112
- project_drift: float32 [2, 768, 768], P(None, ('shard', 'ctx')), may hold values from -20 to 20
- expand_drift: float32 [2, 768, 3072], P(None, ('shard', 'ctx')), may hold values from -40 to 40
- contract_drift: float32 [2, 3072, 768], P(None, ('shard', 'ctx')), may hold values from -28 to 28
- gains_drift: float32 [2, 2, 768], P(None, None, ('shard', 'ctx')), may hold values from -80 to 80
- biases_drift: float32 [2, 11, 768], P(None, None, ('shard', 'ctx')), may hold values from -112 to 112
- attend_spread: float32 [2, 768, 2304], P(None, ('shard', 'ctx')), may hold values from 204.8 to 8192
- project_spread: float32 [2, 768, 768], P(None, ('shard', 'ctx')), may hold values from 4.096 to 81.92
- expand_spread: float32 [2, 768, 3072], P(None, ('shard', 'ctx')), may hold values from 20.48 to 409.6
- contract_spread: float32 [2, 3072, 768], P(None, ('shard', 'ctx')), may hold values from 12.288 to 204.8
- gains_spread: float32 [2, 2, 768], P(None, None, ('shard', 'ctx')), may hold values from 81.92 to 1638.4
- biases_spread: float32 [2, 11, 768], P(None, None, ('shard', 'ctx')), may hold values from 204.8 to 8192
Outputs:
- block_output: float32 [16, 256, 768], P(('rep', 'shard'), 'ctx')
- input_grad: float32 [16, 256, 768], P(('rep', 'shard'), 'ctx')
- attend_grad: float32 [2, 768, 2304], P(None, ('shard', 'ctx'))
- project_grad: float32 [2, 768, 768], P(None, ('shard', 'ctx'))
- expand_grad: float32 [2, 768, 3072], P(None, ('shard', 'ctx'))
- contract_grad: float32 [2, 3072, 768], P(None, ('shard', 'ctx'))
- gains_grad: float32 [2, 2, 768], P(None, None, ('shard', 'ctx'))
- biases_grad: float32 [2, 11, 768], P(None, None, ('shard', 'ctx'))
- attend_next: float32 [2, 768, 2304], P(None, ('shard', 'ctx'))
- project_next: float32 [2, 768, 768], P(None, ('shard', 'ctx'))
- expand_next: float32 [2, 768, 3072], P(None, ('shard', 'ctx'))
- contract_next: float32 [2, 3072, 768], P(None, ('shard', 'ctx'))
- gains_next: float32 [2, 2, 768], P(None, None, ('shard', 'ctx'))
- biases_next: float32 [2, 11, 768], P(None, None, ('shard', 'ctx'))
- moment_attend: float32 [2, 768, 2304], P(None, ('shard', 'ctx'))
- moment_project: float32 [2, 768, 768], P(None, ('shard', 'ctx'))
- moment_expand: float32 [2, 768, 3072], P(None, ('shard', 'ctx'))
- moment_contract: float32 [2, 3072, 768], P(None, ('shard', 'ctx'))
- moment_gains: float32 [2, 2, 768], P(None, None, ('shard', 'ctx'))
- moment_biases: float32 [2, 11, 768], P(None, None, ('shard', 'ctx'))
- square_attend: float32 [2, 768, 2304], P(None, ('shard', 'ctx'))
- square_project: float32 [2, 768, 768], P(None, ('shard', 'ctx'))
- square_expand: float32 [2, 768, 3072], P(None, ('shard', 'ctx'))
- square_contract: float32 [2, 3072, 768], P(None, ('shard', 'ctx'))
- square_gains: float32 [2, 2, 768], P(None, None, ('shard', 'ctx'))
- square_biases: float32 [2, 11, 768], P(None, None, ('shard', 'ctx'))
All inputs are finite; a program needn't handle non-finite values.
Results may differ from a plain program's by a relative error of at most 0.023.
The roundings to bfloat16 on the way count: a program that leaves them out, or rounds other values in their place, can miss the bound.
Values may be sent and summed in bfloat16 or wider, within the bound.
No kernel may reach another device: no remote copies, remote signals or barrier semaphores. Data moves between devices by JAX's collectives and lax.ppermute only.
A program may use at most 256 MiB of HBM per device.

v0:
```python
import jax
import jax.numpy as jnp
from jax import lax
from jax.sharding import PartitionSpec as P

HEAD = 64
ROT = 16
STEP = 3
EPSILON = 1e-05
BETA_ONE = 0.9
BETA_TWO = 0.95
ADAM_FLOOR = 1e-08
RATE_MATRIX = 0.02
RATE_VECTOR = 0.1
DECAY = 0.01
NEGATIVE = -1e30


def narrow_value(array):
    return array.astype(jnp.bfloat16)


def tables(positions):
    inverse = 10000.0 ** (-jnp.arange(0, ROT, 2, dtype=jnp.float32) / ROT)
    angles = positions.astype(jnp.float32)[:, None] * inverse[None, :]
    angles = jnp.concatenate([angles, angles], axis=1)
    return (jnp.cos(angles), jnp.sin(angles))


def split_heads(matrix):
    return matrix.reshape(matrix.shape[0], matrix.shape[1] // HEAD, HEAD)


def rotate(values, cosine, sine):
    half = ROT // 2
    front = values[..., :ROT]
    turned = jnp.concatenate([-front[..., half:], front[..., :half]], axis=-1)
    front = front * cosine[:, None, :] + turned * sine[:, None, :]
    return jnp.concatenate([front, values[..., ROT:]], axis=-1)


def rotate_back(grads, cosine, sine):
    half = ROT // 2
    front = grads[..., :ROT]
    sined = front * sine[:, None, :]
    backward_result = front * cosine[:, None, :] + jnp.concatenate(
        [sined[..., half:], -sined[..., :half]], axis=-1
    )
    return jnp.concatenate([backward_result, grads[..., ROT:]], axis=-1)


def layer_norm_statistics(residual_stream):
    centred = residual_stream - jnp.mean(residual_stream, axis=-1, keepdims=True)
    scale_factor = lax.rsqrt(jnp.mean(centred * centred, axis=-1, keepdims=True) + EPSILON)
    return (centred * scale_factor, scale_factor)


def layer_norm_backward(gradient_tree, normalized_input, scale_factor, gain_vector):
    reshaped_tensor = gradient_tree * gain_vector
    backward_result = (
        reshaped_tensor
        - jnp.mean(reshaped_tensor, axis=-1, keepdims=True)
        - normalized_input * jnp.mean(reshaped_tensor * normalized_input, axis=-1, keepdims=True)
    ) * scale_factor
    return (
        backward_result,
        jnp.sum(gradient_tree * normalized_input, axis=0),
        jnp.sum(gradient_tree, axis=0),
    )


def gelu(inputs):
    return 0.5 * inputs * (1.0 + lax.erf(inputs * 0.7071067811865476))


def gelu_slope(inputs):
    return (
        0.5 * (1.0 + lax.erf(inputs * 0.7071067811865476))
        + inputs * jnp.exp(-0.5 * inputs * inputs) * 0.3989422804014327
    )


def attend_block(carry, query_tensor, positions, piece):
    maximum, total, accum = carry
    keys = split_heads(piece[0])
    values = split_heads(piece[1])
    count = keys.shape[0]
    scores = jnp.einsum(
        "qhd,khd->hqk", query_tensor, keys, preferred_element_type=jnp.float32
    ) * HEAD ** (-0.5)
    allowed = (positions[:, None] >= jnp.arange(count, dtype=jnp.int32)[None, :])[None]
    scores = jnp.where(allowed, scores, NEGATIVE)
    peak = jnp.maximum(maximum, jnp.max(scores, axis=2))
    weights = jnp.where(allowed, jnp.exp(scores - peak[:, :, None]), 0.0)
    total = jnp.sum(weights, axis=2)
    accum = jnp.einsum(
        "hqk,khd->qhd", narrow_value(weights), values, preferred_element_type=jnp.float32
    )
    return (peak, total, accum)


def fetch_weights(shards):
    return (
        lax.all_gather(shards[0], ("shard", "ctx"), axis=0, tiled=True),
        lax.all_gather(shards[1], ("shard", "ctx"), axis=0, tiled=True),
        lax.all_gather(shards[2], ("shard", "ctx"), axis=0, tiled=True),
        lax.all_gather(shards[3], ("shard", "ctx"), axis=0, tiled=True),
        lax.all_gather(shards[4], ("shard", "ctx"), axis=1, tiled=True),
        lax.all_gather(shards[5], ("shard", "ctx"), axis=1, tiled=True),
    )


def sum_grads(local):
    owned = (
        lax.psum_scatter(local[0], ("shard", "ctx"), scatter_dimension=0, tiled=True),
        lax.psum_scatter(local[1], ("shard", "ctx"), scatter_dimension=0, tiled=True),
        lax.psum_scatter(local[2], ("shard", "ctx"), scatter_dimension=0, tiled=True),
        lax.psum_scatter(local[3], ("shard", "ctx"), scatter_dimension=0, tiled=True),
        lax.psum_scatter(local[4], ("shard", "ctx"), scatter_dimension=1, tiled=True),
        lax.psum_scatter(local[5], ("shard", "ctx"), scatter_dimension=1, tiled=True),
    )
    return lax.psum((owned[0], owned[1], owned[2], owned[3], owned[4], owned[5]), "rep")


def layer_forward(residual_stream, params, cosine, sine, positions):
    attend, project, expand, contract, gains, biases = params
    gain_float32 = gains.astype(jnp.float32)
    bias_float32 = biases.astype(jnp.float32)
    span, width = residual_stream.shape
    heads = width // HEAD
    normalized_input, scale_factor = layer_norm_statistics(residual_stream)
    first_normalized = narrow_value(normalized_input * gain_float32[0] + bias_float32[0])
    second_normalized = narrow_value(normalized_input * gain_float32[1] + bias_float32[1])
    mixed = jnp.dot(first_normalized, attend, preferred_element_type=jnp.float32) + bias_float32[
        4:7
    ].reshape(-1)
    query_tensor = narrow_value(rotate(split_heads(mixed[:, :width]), cosine, sine))
    key_rows = narrow_value(
        rotate(split_heads(mixed[:, width : 2 * width]), cosine, sine).reshape(span, width)
    )
    value_rows = narrow_value(mixed[:, 2 * width :])
    start_carry = (
        jnp.full((heads, span), NEGATIVE, jnp.float32),
        jnp.zeros((heads, span), jnp.float32),
        jnp.zeros((span, heads, HEAD), jnp.float32),
    )
    peak, total, accum = attend_block(
        start_carry,
        query_tensor,
        positions,
        (
            lax.all_gather(key_rows, "ctx", axis=0, tiled=True),
            lax.all_gather(value_rows, "ctx", axis=0, tiled=True),
        ),
    )
    context = accum / jnp.transpose(total)[:, :, None]
    log_sum_exp = peak + jnp.log(total)
    context_rows = narrow_value(context.reshape(span, width))
    attn_out = jnp.dot(context_rows, project, preferred_element_type=jnp.float32) + bias_float32[2]
    upper_bound = jnp.dot(
        second_normalized, expand, preferred_element_type=jnp.float32
    ) + bias_float32[7:].reshape(-1)
    active_mask = narrow_value(gelu(upper_bound))
    branch = jnp.dot(active_mask, contract, preferred_element_type=jnp.float32) + bias_float32[3]
    saved_tensors = (
        normalized_input,
        scale_factor,
        first_normalized,
        second_normalized,
        query_tensor,
        key_rows,
        value_rows,
        context_rows,
        log_sum_exp,
        upper_bound,
        active_mask,
        None,
    )
    return (residual_stream + attn_out + branch, saved_tensors)


def layer_backward(grad_out, params, saved_tensors, cosine, sine, positions):
    attend, project, expand, contract, gains, biases = params
    gain_float32 = gains.astype(jnp.float32)
    (
        normalized_input,
        scale_factor,
        first_normalized,
        second_normalized,
        query_tensor,
        key_rows,
        value_rows,
        context_rows,
        log_sum_exp,
        upper_bound,
        active_mask,
        full_keys,
    ) = saved_tensors
    span, width = grad_out.shape
    grad_b = narrow_value(grad_out)
    grad_contract = jnp.dot(active_mask.T, grad_b, preferred_element_type=jnp.float32)
    grad_project = jnp.dot(context_rows.T, grad_b, preferred_element_type=jnp.float32)
    grad_up = jnp.dot(grad_b, contract.T, preferred_element_type=jnp.float32) * gelu_slope(
        upper_bound
    )
    up_bias_gradient = narrow_value(grad_up)
    grad_context = split_heads(
        narrow_value(jnp.dot(grad_b, project.T, preferred_element_type=jnp.float32))
    )
    grad_expand = jnp.dot(second_normalized.T, up_bias_gradient, preferred_element_type=jnp.float32)
    second_backward, second_gain, second_shift = layer_norm_backward(
        jnp.dot(up_bias_gradient, expand.T, preferred_element_type=jnp.float32),
        normalized_input,
        scale_factor,
        gain_float32[1],
    )
    keys_all, values_all = (
        lax.all_gather(key_rows, "ctx", axis=0, tiled=True),
        lax.all_gather(value_rows, "ctx", axis=0, tiled=True),
    )
    length = keys_all.shape[0]
    keys = split_heads(keys_all)
    values = split_heads(values_all)
    delta = jnp.einsum(
        "qhd,qhd->hq", grad_context, split_heads(context_rows), preferred_element_type=jnp.float32
    )
    scores = jnp.einsum(
        "qhd,khd->hqk", query_tensor, keys, preferred_element_type=jnp.float32
    ) * HEAD ** (-0.5)
    allowed = (positions[:, None] >= jnp.arange(length, dtype=jnp.int32)[None, :])[None]
    probs = jnp.where(
        allowed, jnp.exp(jnp.where(allowed, scores, NEGATIVE) - log_sum_exp[:, :, None]), 0.0
    )
    grad_probs = jnp.einsum(
        "qhd,khd->hqk", grad_context, values, preferred_element_type=jnp.float32
    )
    grad_scores = narrow_value(probs * (grad_probs - delta[:, :, None]) * HEAD ** (-0.5))
    grad_query = jnp.einsum("hqk,khd->qhd", grad_scores, keys, preferred_element_type=jnp.float32)
    key_terms = jnp.einsum(
        "hqk,qhd->khd", grad_scores, query_tensor, preferred_element_type=jnp.float32
    ).reshape(length, width)
    value_terms = jnp.einsum(
        "hqk,qhd->khd", narrow_value(probs), grad_context, preferred_element_type=jnp.float32
    ).reshape(length, width)
    grad_key, grad_value = (
        lax.psum_scatter(key_terms, "ctx", scatter_dimension=0, tiled=True),
        lax.psum_scatter(value_terms, "ctx", scatter_dimension=0, tiled=True),
    )
    grad_mixed = jnp.concatenate(
        [
            rotate_back(grad_query, cosine, sine).reshape(span, width),
            rotate_back(split_heads(grad_key), cosine, sine).reshape(span, width),
            grad_value,
        ],
        axis=1,
    )
    mixed_bias_gradient = narrow_value(grad_mixed)
    grad_attend = jnp.dot(
        first_normalized.T, mixed_bias_gradient, preferred_element_type=jnp.float32
    )
    first_backward, first_gain, first_shift = layer_norm_backward(
        jnp.dot(mixed_bias_gradient, attend.T, preferred_element_type=jnp.float32),
        normalized_input,
        scale_factor,
        gain_float32[0],
    )
    grad_in = grad_out + first_backward + second_backward
    column = jnp.sum(grad_out, axis=0)
    grad_gains = jnp.stack([first_gain, second_gain])
    grad_biases = jnp.concatenate(
        [
            jnp.stack([first_shift, second_shift, column, column]),
            jnp.sum(grad_mixed, axis=0).reshape(3, width),
            jnp.sum(grad_up, axis=0).reshape(-1, width),
        ],
        axis=0,
    )
    return (
        grad_in,
        (grad_attend, grad_project, grad_expand, grad_contract, grad_gains, grad_biases),
    )


def adam_step(weight, gradient_tree, drift, spread, rate):
    drift_new = BETA_ONE * drift + (1.0 - BETA_ONE) * gradient_tree
    spread_new = BETA_TWO * spread + (1.0 - BETA_TWO) * gradient_tree * gradient_tree
    mean_hat = drift_new / (1.0 - BETA_ONE**STEP)
    square_hat = spread_new / (1.0 - BETA_TWO**STEP)
    weight_new = weight - rate * (mean_hat / (jnp.sqrt(square_hat) + ADAM_FLOOR) + DECAY * weight)
    return (weight_new, drift_new, spread_new)


def body(
    block_input,
    cotangent,
    attend,
    project,
    expand,
    contract,
    gains,
    biases,
    attend_drift,
    project_drift,
    expand_drift,
    contract_drift,
    gains_drift,
    biases_drift,
    attend_spread,
    project_spread,
    expand_spread,
    contract_spread,
    gains_spread,
    biases_spread,
):
    span = block_input.shape[1]
    layers = attend.shape[0]
    positions = lax.axis_index("ctx") * span + jnp.arange(span, dtype=jnp.int32)
    cosine, sine = tables(positions)
    masters = (attend, project, expand, contract, gains, biases)
    residual_stream = block_input[0].astype(jnp.float32)
    params_all = []
    saved_all = []
    for layer in range(layers):
        params = fetch_weights(tuple((narrow_value(master[layer]) for master in masters)))
        residual_stream, saved_tensors = layer_forward(
            residual_stream, params, cosine, sine, positions
        )
        params_all.append(params)
        saved_all.append(saved_tensors)
    gradient_tree = cotangent[0].astype(jnp.float32)
    grads_all = [None] * layers
    for layer in reversed(range(layers)):
        gradient_tree, local = layer_backward(
            gradient_tree, params_all[layer], saved_all[layer], cosine, sine, positions
        )
        grads_all[layer] = sum_grads(local)
    totals = tuple(
        (jnp.stack([grads_all[layer][index] for layer in range(layers)]) for index in range(6))
    )
    drifts = (attend_drift, project_drift, expand_drift, contract_drift, gains_drift, biases_drift)
    spreads = (
        attend_spread,
        project_spread,
        expand_spread,
        contract_spread,
        gains_spread,
        biases_spread,
    )
    rates = (RATE_MATRIX, RATE_MATRIX, RATE_MATRIX, RATE_MATRIX, RATE_VECTOR, RATE_VECTOR)
    updated = [
        adam_step(masters[index], totals[index], drifts[index], spreads[index], rates[index])
        for index in range(6)
    ]
    return (
        residual_stream[None],
        gradient_tree[None],
        totals[0],
        totals[1],
        totals[2],
        totals[3],
        totals[4],
        totals[5],
        updated[0][0],
        updated[1][0],
        updated[2][0],
        updated[3][0],
        updated[4][0],
        updated[5][0],
        updated[0][1],
        updated[1][1],
        updated[2][1],
        updated[3][1],
        updated[4][1],
        updated[5][1],
        updated[0][2],
        updated[1][2],
        updated[2][2],
        updated[3][2],
        updated[4][2],
        updated[5][2],
    )


def solution(mesh):
    in_specs = (
        P(("rep", "shard"), "ctx", None),
        P(("rep", "shard"), "ctx", None),
        P(None, ("shard", "ctx"), None),
        P(None, ("shard", "ctx"), None),
        P(None, ("shard", "ctx"), None),
        P(None, ("shard", "ctx"), None),
        P(None, None, ("shard", "ctx")),
        P(None, None, ("shard", "ctx")),
        P(None, ("shard", "ctx"), None),
        P(None, ("shard", "ctx"), None),
        P(None, ("shard", "ctx"), None),
        P(None, ("shard", "ctx"), None),
        P(None, None, ("shard", "ctx")),
        P(None, None, ("shard", "ctx")),
        P(None, ("shard", "ctx"), None),
        P(None, ("shard", "ctx"), None),
        P(None, ("shard", "ctx"), None),
        P(None, ("shard", "ctx"), None),
        P(None, None, ("shard", "ctx")),
        P(None, None, ("shard", "ctx")),
    )
    out_specs = (
        P(("rep", "shard"), "ctx", None),
        P(("rep", "shard"), "ctx", None),
        P(None, ("shard", "ctx"), None),
        P(None, ("shard", "ctx"), None),
        P(None, ("shard", "ctx"), None),
        P(None, ("shard", "ctx"), None),
        P(None, None, ("shard", "ctx")),
        P(None, None, ("shard", "ctx")),
        P(None, ("shard", "ctx"), None),
        P(None, ("shard", "ctx"), None),
        P(None, ("shard", "ctx"), None),
        P(None, ("shard", "ctx"), None),
        P(None, None, ("shard", "ctx")),
        P(None, None, ("shard", "ctx")),
        P(None, ("shard", "ctx"), None),
        P(None, ("shard", "ctx"), None),
        P(None, ("shard", "ctx"), None),
        P(None, ("shard", "ctx"), None),
        P(None, None, ("shard", "ctx")),
        P(None, None, ("shard", "ctx")),
        P(None, ("shard", "ctx"), None),
        P(None, ("shard", "ctx"), None),
        P(None, ("shard", "ctx"), None),
        P(None, ("shard", "ctx"), None),
        P(None, None, ("shard", "ctx")),
        P(None, None, ("shard", "ctx")),
    )
    return jax.shard_map(body, mesh=mesh, in_specs=in_specs, out_specs=out_specs, check_vma=False)
```

profile of v0, /device:TPU:0, one launch (start us, length us, event | category | flops | bytes accessed | tf_op | source)
XLA Modules:
  0.0 2157.8 jit_solution(18050966352097046684)
XLA Ops:
  19.1 33.3 %all-gather = bf16[1,2,768]{1,0,2:T(2,128)(2,1)S(1)} all-gather(bf16[1,2,96]{1,0,2:T(2,128)(2,1)S(1)} %get-tuple-element.200), channel_id=2, replica_groups=mesh['rep'=4,'shard'=4,'ctx'=2] {'shard','ctx'}, dimensions={2}, use_global_device_ids=true | all-gather | bytes 3456 | tf_op jit(solution)/shard_map/all_gather | solution.py:108
  58.0 32.0 %all-gather.6 = bf16[1,2,768]{1,0,2:T(2,128)(2,1)S(1)} all-gather(bf16[1,2,96]{1,0,2:T(2,128)(2,1)S(1)} %get-tuple-element.201), channel_id=8, replica_groups=mesh['rep'=4,'shard'=4,'ctx'=2] {'shard','ctx'}, dimensions={2}, use_global_device_ids=true | all-gather | bytes 3456 | tf_op jit(solution)/shard_map/all_gather | solution.py:108
  95.7 33.0 %all-gather.7 = bf16[1,11,768]{1,0,2:T(2,128)(2,1)S(1)} all-gather(bf16[1,11,96]{1,0,2:T(2,128)(2,1)S(1)} %get-tuple-element.203), channel_id=9, replica_groups=mesh['rep'=4,'shard'=4,'ctx'=2] {'shard','ctx'}, dimensions={2}, use_global_device_ids=true | all-gather | bytes 19008 | tf_op jit(solution)/shard_map/all_gather | solution.py:109
  130.0 43.3 %all-gather.1 = bf16[1,11,768]{1,0,2:T(2,128)(2,1)S(1)} all-gather(bf16[1,11,96]{1,0,2:T(2,128)(2,1)S(1)} %get-tuple-element.202), channel_id=3, replica_groups=mesh['rep'=4,'shard'=4,'ctx'=2] {'shard','ctx'}, dimensions={2}, use_global_device_ids=true | all-gather | bytes 19008 | tf_op jit(solution)/shard_map/all_gather | solution.py:109
  177.6 10.9 slice_reduce_fusion.3
  188.5 11.3 slice_reduce_fusion.9
  205.4 6.3 all_gather.55
  212.3 6.4 all_gather.56
  224.2 73.3 %all-gather.27.cloned.1.call-done = bf16[1,3072,768]{2,1,0:T(8,128)(2,1)} async-done(((bf16[1,384,768]{2,1,0:T(8,128)(2,1)}), bf16[1,3072,768]{2,1,0:T(8,128)(2,1)}) %all-gather.27.cloned.1.call-update) | async-done | bytes 4718608 | tf_op jit(solution)/shard_map/all_gather | solution.py:107
  300.9 38.8 %all-gather.23.cloned.1.call-done = bf16[1,768,768]{2,1,0:T(8,128)(2,1)} async-done(((bf16[1,96,768]{2,1,0:T(8,128)(2,1)}), bf16[1,768,768]{2,1,0:T(8,128)(2,1)}) %all-gather.23.cloned.1.call-update) | async-done | bytes 1179664 | tf_op jit(solution)/shard_map/all_gather | solution.py:105
  341.7 64.0 %all-gather.29.cloned.1.call-done = bf16[1,768,2304]{2,1,0:T(8,128)(2,1)} async-done(((bf16[1,96,2304]{2,1,0:T(8,128)(2,1)}), bf16[1,768,2304]{2,1,0:T(8,128)(2,1)}) %all-gather.29.cloned.1.call-update) | async-done | bytes 3538960 | tf_op jit(solution)/shard_map/all_gather | solution.py:104
  409.3 6.3 all_gather.63
  416.8 11.0 all_gather.64
  444.1 42.9 %all-gather.33.cloned.1.call-done = bf16[1,768,3072]{2,1,0:T(8,128)(2,1)} async-done(((bf16[1,96,3072]{2,1,0:T(8,128)(2,1)}), bf16[1,768,3072]{2,1,0:T(8,128)(2,1)}) %all-gather.33.cloned.1.call-update) | async-done | bytes 4718608 | tf_op jit(solution)/shard_map/all_gather | solution.py:106
  490.3 77.2 %all-gather.35.cloned.1.call-done = bf16[1,3072,768]{2,1,0:T(8,128)(2,1)} async-done(((bf16[1,384,768]{2,1,0:T(8,128)(2,1)}), bf16[1,3072,768]{2,1,0:T(8,128)(2,1)}) %all-gather.35.cloned.1.call-update) | async-done | bytes 4718608 | tf_op jit(solution)/shard_map/all_gather | solution.py:107
  576.0 10.3 reduce-scatter.25.cloned.1.call-done
  590.8 15.6 reduce-scatter.27.cloned.1.call-done
  644.3 15.6 reduce-scatter.31.cloned.1.call-done
  708.7 25.0 %reduce-scatter.39.cloned.1.call-done = f32[96,768]{1,0:T(8,128)} async-done(((f32[768,768]{1,0:T(8,128)}), f32[96,768]{1,0:T(8,128)}) %reduce-scatter.39.cloned.1.call-update) | async-done | bytes 294928 | tf_op jit(solution)/shard_map/reduce_scatter | solution.py:116
  733.7 72.8 %reduce-scatter.37.cloned.1.call-done = f32[96,768]{1,0:T(8,128)} async-done(((f32[768,768]{1,0:T(8,128)}), f32[96,768]{1,0:T(8,128)}) %reduce-scatter.37.cloned.1.call-update) | async-done | bytes 294928 | tf_op jit(solution)/shard_map/reduce_scatter | solution.py:116
  806.5 131.9 %reduce-scatter.35.cloned.1.call-done = f32[96,2304]{1,0:T(8,128)} async-done(((f32[768,2304]{1,0:T(8,128)}), f32[96,2304]{1,0:T(8,128)}) %reduce-scatter.35.cloned.1.call-update) | async-done | bytes 884752 | tf_op jit(solution)/shard_map/reduce_scatter | solution.py:115
  938.4 131.8 %reduce-scatter.33.cloned.1.call-done = f32[96,2304]{1,0:T(8,128)} async-done(((f32[768,2304]{1,0:T(8,128)}), f32[96,2304]{1,0:T(8,128)}) %reduce-scatter.33.cloned.1.call-update) | async-done | bytes 884752 | tf_op jit(solution)/shard_map/reduce_scatter | solution.py:115
  1070.2 164.7 %reduce-scatter.47.cloned.1.call-done = f32[384,768]{1,0:T(8,128)} async-done(((f32[3072,768]{1,0:T(8,128)}), f32[384,768]{1,0:T(8,128)}) %reduce-scatter.47.cloned.1.call-update) | async-done | bytes 1179664 | tf_op jit(solution)/shard_map/reduce_scatter | solution.py:118
  1234.9 164.7 %reduce-scatter.43.cloned.1.call-done = f32[96,3072]{1,0:T(8,128)} async-done(((f32[768,3072]{1,0:T(8,128)}), f32[96,3072]{1,0:T(8,128)}) %reduce-scatter.43.cloned.1.call-update) | async-done | bytes 1179664 | tf_op jit(solution)/shard_map/reduce_scatter | solution.py:117
  1399.6 164.8 %reduce-scatter.45.cloned.1.call-done = f32[384,768]{1,0:T(8,128)} async-done(((f32[3072,768]{1,0:T(8,128)}), f32[384,768]{1,0:T(8,128)}) %reduce-scatter.45.cloned.1.call-update) | async-done | bytes 1179664 | tf_op jit(solution)/shard_map/reduce_scatter | solution.py:118
  1564.4 164.7 %reduce-scatter.41.cloned.1.call-done = f32[96,3072]{1,0:T(8,128)} async-done(((f32[768,3072]{1,0:T(8,128)}), f32[96,3072]{1,0:T(8,128)}) %reduce-scatter.41.cloned.1.call-update) | async-done | bytes 1179664 | tf_op jit(solution)/shard_map/reduce_scatter | solution.py:117
  1734.4 60.0 %reduce-scatter.51.cloned.1.call-done = f32[96,2]{1,0:T(8,128)} async-done(((f32[768,2]{1,0:T(8,128)}), f32[96,2]{1,0:T(8,128)}) %reduce-scatter.51.cloned.1.call-update) | async-done | bytes 784
  1795.2 64.3 %reduce-scatter.55.cloned.1.call-done = f32[96,11]{1,0:T(8,128)} async-done(((f32[768,11]{1,0:T(8,128)}), f32[96,11]{1,0:T(8,128)}) %reduce-scatter.55.cloned.1.call-update) | async-done | bytes 4240
  1861.5 63.2 %reduce-scatter.49.cloned.1.call-done = f32[96,2]{1,0:T(8,128)} async-done(((f32[768,2]{1,0:T(8,128)}), f32[96,2]{1,0:T(8,128)}) %reduce-scatter.49.cloned.1.call-update) | async-done | bytes 784
  1925.5 64.1 %reduce-scatter.53.cloned.1.call-done = f32[96,11]{1,0:T(8,128)} async-done(((f32[768,11]{1,0:T(8,128)}), f32[96,11]{1,0:T(8,128)}) %reduce-scatter.53.cloned.1.call-update) | async-done | bytes 4240
  1990.5 10.9 all-reduce
  2004.5 119.6 %all-reduce.4.cloned.1.call-done = (f32[1,96,2304]{2,1,0:T(8,128)}, f32[1,96,2304]{2,1,0:T(8,128)}, f32[1,96,768]{2,1,0:T(8,128)}, f32[1,96,768]{2,1,0:T(8,128)}...) async-done(((f32[1,96,2304]{2,1,0:T(8,128)}, f32[1,96,2304]{2,1,0:T(8,128)}, f32[1,96,768]{2,1,0:T(8,128)}, ...) | async-done | bytes 7077904 | tf_op jit(solution)/shard_map/psum | solution.py:122
  (486 shorter events, 207.5 us)
Async XLA Ops:
  7.2 192.5 %all-gather.31.cloned.1.call-start = ((), (), s32[]{:S(2)}) async-start(), calls=%async_computation.33 | async-start | bytes 1327104 | tf_op jit(solution)/shard_map/all_gather | solution.py:105
  9.1 193.3 %all-gather.21.cloned.1.call-start = ((), (), s32[]{:S(2)}) async-start(), calls=%async_computation.28 | async-start | bytes 3981312 | tf_op jit(solution)/shard_map/all_gather | solution.py:104
  11.9 209.0 %all-gather.25.cloned.1.call-start = ((), (), s32[]{:S(2)}) async-start(), calls=%async_computation.30 | async-start | bytes 5308416 | tf_op jit(solution)/shard_map/all_gather | solution.py:106
  13.2 284.4 %all-gather.27.cloned.1.call-start = ((), (), s32[]{:S(2)}) async-start(), calls=%async_computation.31 | async-start | bytes 5308416 | tf_op jit(solution)/shard_map/all_gather | solution.py:107
  15.4 324.3 %all-gather.23.cloned.1.call-start = ((), (), s32[]{:S(2)}) async-start(), calls=%async_computation.29 | async-start | bytes 1327104 | tf_op jit(solution)/shard_map/all_gather | solution.py:105
  16.0 389.6 %all-gather.29.cloned.1.call-start = ((), (), s32[]{:S(2)}) async-start(), calls=%async_computation.32 | async-start | bytes 3981312 | tf_op jit(solution)/shard_map/all_gather | solution.py:104
  16.6 470.4 %all-gather.33.cloned.1.call-start = ((), (), s32[]{:S(2)}) async-start(), calls=%async_computation.34 | async-start | bytes 5308416 | tf_op jit(solution)/shard_map/all_gather | solution.py:106
  17.3 550.2 %all-gather.35.cloned.1.call-start = ((), (), s32[]{:S(2)}) async-start(), calls=%async_computation.35 | async-start | bytes 5308416 | tf_op jit(solution)/shard_map/all_gather | solution.py:107
  18.1 568.1 %reduce-scatter.25.cloned.1.call-start = ((), (), s32[]{:S(2)}) async-start(), calls=%async_computation.16 | async-start | bytes 1179648 | tf_op jit(solution)/shard_map/reduce_scatter | solution.py:246
  18.6 201.1 %copy-start.44 = (pred[128,256]{1,0:T(8,128)(4,1)}, pred[128,256]{1,0:T(8,128)(4,1)S(1)}, u32[]{:S(2)}) copy-start(pred[128,256]{1,0:T(8,128)(4,1)S(1)} %iota_compare_fusion) | copy-start | bytes 98308
  434.7 171.7 %reduce-scatter.27.cloned.1.call-start = ((), (), s32[]{:S(2)}) async-start(), calls=%async_computation.17 | async-start | bytes 1179648 | tf_op jit(solution)/shard_map/reduce_scatter | solution.py:247
  444.1 195.6 %reduce-scatter.29.cloned.1.call-start = ((), (), s32[]{:S(2)}) async-start(), calls=%async_computation.18 | async-start | bytes 1179648 | tf_op jit(solution)/shard_map/reduce_scatter | solution.py:246
  622.0 37.9 %reduce-scatter.31.cloned.1.call-start = ((), (), s32[]{:S(2)}) async-start(), calls=%async_computation.19 | async-start | bytes 1179648 | tf_op jit(solution)/shard_map/reduce_scatter | solution.py:247
  624.8 108.9 %reduce-scatter.39.cloned.1.call-start = ((), (), s32[]{:S(2)}) async-start(), calls=%async_computation.23 | async-start | bytes 2654208 | tf_op jit(solution)/shard_map/reduce_scatter | solution.py:116
  627.8 178.7 %reduce-scatter.37.cloned.1.call-start = ((), (), s32[]{:S(2)}) async-start(), calls=%async_computation.22 | async-start | bytes 2654208 | tf_op jit(solution)/shard_map/reduce_scatter | solution.py:116
  630.7 307.7 %reduce-scatter.35.cloned.1.call-start = ((), (), s32[]{:S(2)}) async-start(), calls=%async_computation.21 | async-start | bytes 7962624 | tf_op jit(solution)/shard_map/reduce_scatter | solution.py:115
  636.3 433.9 %reduce-scatter.33.cloned.1.call-start = ((), (), s32[]{:S(2)}) async-start(), calls=%async_computation.20 | async-start | bytes 7962624 | tf_op jit(solution)/shard_map/reduce_scatter | solution.py:115
  665.3 569.6 %reduce-scatter.47.cloned.1.call-start = ((), (), s32[]{:S(2)}) async-start(), calls=%async_computation.27 | async-start | bytes 10616832 | tf_op jit(solution)/shard_map/reduce_scatter | solution.py:118
  671.4 728.2 %reduce-scatter.43.cloned.1.call-start = ((), (), s32[]{:S(2)}) async-start(), calls=%async_computation.25 | async-start | bytes 10616832 | tf_op jit(solution)/shard_map/reduce_scatter | solution.py:117
  678.4 886.0 %reduce-scatter.45.cloned.1.call-start = ((), (), s32[]{:S(2)}) async-start(), calls=%async_computation.26 | async-start | bytes 10616832 | tf_op jit(solution)/shard_map/reduce_scatter | solution.py:118
  684.5 1044.6 %reduce-scatter.41.cloned.1.call-start = ((), (), s32[]{:S(2)}) async-start(), calls=%async_computation.24 | async-start | bytes 10616832 | tf_op jit(solution)/shard_map/reduce_scatter | solution.py:117
  695.7 1098.6 %reduce-scatter.51.cloned.1.call-start = ((), (), s32[]{:S(2)}) async-start(), calls=%async_computation.37 | async-start | bytes 442368
  697.4 1162.2 %reduce-scatter.55.cloned.1.call-start = ((), (), s32[]{:S(2)}) async-start(), calls=%async_computation.39 | async-start | bytes 442368
  699.1 1225.6 %reduce-scatter.49.cloned.1.call-start = ((), (), s32[]{:S(2)}) async-start(), calls=%async_computation.36 | async-start | bytes 442368
  707.1 1282.5 %reduce-scatter.53.cloned.1.call-start = ((), (), s32[]{:S(2)}) async-start(), calls=%async_computation.38 | async-start | bytes 442368
  708.7 1415.4 %all-reduce.4.cloned.1.call-start = ((), (), s32[]{:S(2)}) async-start(), calls=%async_computation.40 | async-start | bytes 14155776 | tf_op jit(solution)/shard_map/psum | solution.py:122
  1734.3 267.7 %copy-start.88 = (f32[2,11,96]{2,0,1:T(2,128)S(1)}, f32[2,11,96]{2,0,1:T(2,128)}, u32[]{:S(2)}) copy-start(f32[2,11,96]{2,0,1:T(2,128)} %param.27) | copy-start | bytes 25348
  1734.3 267.7 %copy-start.111 = (f32[2,11,96]{2,0,1:T(2,128)S(1)}, f32[2,11,96]{2,0,1:T(2,128)}, u32[]{:S(2)}) copy-start(f32[2,11,96]{2,0,1:T(2,128)} %param.33) | copy-start | bytes 25348
  1734.3 267.7 %copy-start.112 = (f32[2,11,96]{2,0,1:T(2,128)S(1)}, f32[2,11,96]{2,0,1:T(2,128)}, u32[]{:S(2)}) copy-start(f32[2,11,96]{2,0,1:T(2,128)} %param.39) | copy-start | bytes 25348
  1734.3 269.5 %copy-start.114 = (f32[2,2,96]{2,1,0:T(2,128)S(1)}, f32[2,2,96]{2,1,0:T(2,128)}, u32[]{:S(2)}) copy-start(f32[2,2,96]{2,1,0:T(2,128)} %param.26) | copy-start | bytes 4612
  1734.3 269.5 %copy-start.120 = (f32[2,2,96]{2,1,0:T(2,128)S(1)}, f32[2,2,96]{2,1,0:T(2,128)}, u32[]{:S(2)}) copy-start(f32[2,2,96]{2,1,0:T(2,128)} %param.32) | copy-start | bytes 4612
  1734.4 269.5 %copy-start.121 = (f32[2,2,96]{2,1,0:T(2,128)S(1)}, f32[2,2,96]{2,1,0:T(2,128)}, u32[]{:S(2)}) copy-start(f32[2,2,96]{2,1,0:T(2,128)} %param.38) | copy-start | bytes 4612
  (117 other events, 2124.0 us)
Sparse Core Ops, SparseCore 0:
  10.8 45.3 all-gather.30
  58.9 71.3 all-gather.20
  133.1 84.1 all-gather.24
  219.8 77.6 all-gather.26
  300.2 39.4 all-gather.22
  342.3 63.2 all-gather.28
  408.4 78.5 all-gather.32
  489.8 77.6 all-gather.34
  570.3 15.8 reduce-scatter.24
  588.9 17.4 reduce-scatter.26
  622.1 17.5 reduce-scatter.28
  642.3 17.4 reduce-scatter.30
  663.9 69.7 reduce-scatter.38
  737.7 68.7 reduce-scatter.36
  810.0 128.3 reduce-scatter.34
  941.9 128.2 reduce-scatter.32
  1073.7 161.2 reduce-scatter.46
  1238.4 161.2 reduce-scatter.42
  1403.2 161.1 reduce-scatter.44
  1567.9 161.1 reduce-scatter.40
  1733.0 61.3 reduce-scatter.50
  1798.2 61.2 reduce-scatter.54
  1863.4 61.2 reduce-scatter.48
  1928.4 61.2 reduce-scatter.52
  1992.5 131.5 all-reduce.3
where the time goes:
time: 2170 us; the launch traced here: 2160 us
  waiting for transfers between devices  1730 us (80%)
  blocking collectives  183 us (8%)
  matrix products  104 us (5%)
  local copies, waits for them, and re-layouts  87.5 us (4%)
  other arithmetic  33 us (2%)
    reduce_scatter x2, waiting for transfers between devices, sum_grads(): lax.psum_scatter(local[3], ('shard', 'ctx'), scatter_dimension=0, tiled=T...  330 us
    reduce_scatter x2, waiting for transfers between devices, sum_grads(): lax.psum_scatter(local[2], ('shard', 'ctx'), scatter_dimension=0, tiled=T...  329 us
    reduce_scatter x2, waiting for transfers between devices, sum_grads(): lax.psum_scatter(local[0], ('shard', 'ctx'), scatter_dimension=0, tiled=T...  264 us
    unnamed x29, waiting for transfers between devices  254 us
    all_gather x2, waiting for transfers between devices, fetch_weights(): lax.all_gather(shards[3], ('shard', 'ctx'), axis=0, tiled=True)  151 us
    psum x1, waiting for transfers between devices, sum_grads(): lax.psum((owned[0], owned[1], owned[2], owned[3], owned[4], owned[5]), 'r...  120 us
    reduce_scatter x2, waiting for transfers between devices, sum_grads(): lax.psum_scatter(local[1], ('shard', 'ctx'), scatter_dimension=0, tiled=T...  97.7 us
    all_gather x2, blocking collectives, fetch_weights(): lax.all_gather(shards[5], ('shard', 'ctx'), axis=1, tiled=True)  76.3 us
  transfers between devices with their start and end apart: 25, of which 22 were waited for; matrix products, arithmetic and copies ran while one was open for 8% of the time, Pallas kernels for 0%

commit v1 on v0

--- a/solution.py
+++ b/solution.py
@@ -14,6 +14,19 @@
 RATE_VECTOR = 0.1
 DECAY = 0.01
 NEGATIVE = -1e30
+
+
+def collect(x, axis, dim):
+    devices, index, rows = (lax.axis_size(axis), lax.axis_index(axis), x.shape[dim])
+    upward = [(i, (i + 1) % devices) for i in range(devices)]
+    out = jnp.zeros((*x.shape[:dim], devices * rows, *x.shape[dim + 1 :]), x.dtype)
+    held = x
+    for step in range(devices):
+        holder = (index - step) % devices
+        out = lax.dynamic_update_slice_in_dim(out, held, holder * rows, axis=dim)
+        if step < devices - 1:
+            held = lax.ppermute(held, axis, upward)
+    return out
 
 
 def narrow_value(array):
@@ -104,7 +117,7 @@
         lax.all_gather(shards[0], ("shard", "ctx"), axis=0, tiled=True),
         lax.all_gather(shards[1], ("shard", "ctx"), axis=0, tiled=True),
         lax.all_gather(shards[2], ("shard", "ctx"), axis=0, tiled=True),
-        lax.all_gather(shards[3], ("shard", "ctx"), axis=0, tiled=True),
+        collect(shards[3], ("shard", "ctx"), 0),
         lax.all_gather(shards[4], ("shard", "ctx"), axis=1, tiled=True),
         lax.all_gather(shards[5], ("shard", "ctx"), axis=1, tiled=True),
     )

time: 2170 us -> 2100 us (0.968)
  waiting for transfers between devices: 1730 us -> 1590 us
  blocking collectives: 183 us -> 225 us
    all_gather x2 -> x0, waiting for transfers between devices: 151 us -> none  [fetch_weights(): lax.all_gather(shards[3], ('shard', 'ctx'), axis=0, tiled=True)]
    ppermute x0 -> x14, waiting for transfers between devices: none -> 127 us  [collect(): held = lax.ppermute(held, axis, upward)]
    all_gather x2, waiting for transfers between devices: 64 us -> 0.02 us  [fetch_weights(): lax.all_gather(shards[0], ('shard', 'ctx'), axis=0, tiled=True)]
    all_gather x2, waiting for transfers between devices: 38.8 us -> 0.02 us  [fetch_weights(): lax.all_gather(shards[1], ('shard', 'ctx'), axis=0, tiled=True)]
    unnamed x29 -> x27, waiting for transfers between devices: 254 us -> 252 us
  transfers between devices with their start and end apart: 25 -> 37, of which waited for: 22 -> 27; matrix products, arithmetic and copies ran while one was open for 8% -> 10% of each run, Pallas kernels for 0% -> 0%
where the time goes in v1:
time: 2100 us; the launch traced here: 2090 us
  waiting for transfers between devices  1590 us (76%)
  blocking collectives  225 us (11%)
  local copies, waits for them, and re-layouts  109 us (5%)
  matrix products  108 us (5%)
  other arithmetic  33.8 us (2%)
    reduce_scatter x2, waiting for transfers between devices, sum_grads(): lax.psum_scatter(local[2], ('shard', 'ctx'), scatter_dimension=0, tiled=T...  329 us
    reduce_scatter x2, waiting for transfers between devices, sum_grads(): lax.psum_scatter(local[3], ('shard', 'ctx'), scatter_dimension=0, tiled=T...  329 us
    reduce_scatter x2, waiting for transfers between devices, sum_grads(): lax.psum_scatter(local[0], ('shard', 'ctx'), scatter_dimension=0, tiled=T...  264 us
    unnamed x27, waiting for transfers between devices  252 us
    ppermute x14, waiting for transfers between devices, collect(): held = lax.ppermute(held, axis, upward)  127 us
    psum x1, waiting for transfers between devices, sum_grads(): lax.psum((owned[0], owned[1], owned[2], owned[3], owned[4], owned[5]), 'r...  119 us
    reduce_scatter x2, waiting for transfers between devices, sum_grads(): lax.psum_scatter(local[1], ('shard', 'ctx'), scatter_dimension=0, tiled=T...  97.4 us
    all_gather x2, blocking collectives, fetch_weights(): lax.all_gather(shards[5], ('shard', 'ctx'), axis=1, tiled=True)  90.4 us
  transfers between devices with their start and end apart: 37, of which 27 were waited for; matrix products, arithmetic and copies ran while one was open for 10% of the time, Pallas kernels for 0%

profile of v1, /device:TPU:0, one launch (start us, length us, event | category | flops | bytes accessed | tf_op | source)
XLA Modules:
  0.0 2094.4 jit_solution(7861871159544097235)
XLA Ops:
  22.3 57.5 %all-gather.1 = bf16[1,11,768]{1,0,2:T(2,128)(2,1)S(1)} all-gather(bf16[1,11,96]{1,0,2:T(2,128)(2,1)S(1)} %get-tuple-element.203), channel_id=3, replica_groups=mesh['rep'=4,'shard'=4,'ctx'=2] {'shard','ctx'}, dimensions={2}, use_global_device_ids=true | all-gather | bytes 19008 | tf_op jit(solution)/shard_map/all_gather | solution.py:122
  80.4 32.3 %all-gather = bf16[1,2,768]{1,0,2:T(2,128)(2,1)S(1)} all-gather(bf16[1,2,96]{1,0,2:T(2,128)(2,1)S(1)} %get-tuple-element.201), channel_id=2, replica_groups=mesh['rep'=4,'shard'=4,'ctx'=2] {'shard','ctx'}, dimensions={2}, use_global_device_ids=true | all-gather | bytes 3456 | tf_op jit(solution)/shard_map/all_gather | solution.py:121
  113.2 32.9 %all-gather.6 = bf16[1,11,768]{1,0,2:T(2,128)(2,1)S(1)} all-gather(bf16[1,11,96]{1,0,2:T(2,128)(2,1)S(1)} %get-tuple-element.202), channel_id=8, replica_groups=mesh['rep'=4,'shard'=4,'ctx'=2] {'shard','ctx'}, dimensions={2}, use_global_device_ids=true | all-gather | bytes 19008 | tf_op jit(solution)/shard_map/all_gather | solution.py:122
  151.5 18.1 collective-permute-done.1
  170.2 10.9 slice_reduce_fusion.7
  187.2 18.4 collective-permute-done.2
  205.8 10.9 slice_reduce_fusion.1
  226.5 14.1 collective-permute-done.3
  246.6 50.1 %all-gather.5 = bf16[1,2,768]{1,0,2:T(2,128)(2,1)S(1)} all-gather(bf16[1,2,96]{1,0,2:T(2,128)(2,1)S(1)} %get-tuple-element.200), channel_id=7, replica_groups=mesh['rep'=4,'shard'=4,'ctx'=2] {'shard','ctx'}, dimensions={2}, use_global_device_ids=true | all-gather | bytes 3456 | tf_op jit(solution)/shard_map/all_gather | solution.py:121
  311.7 21.3 %collective-permute-done.11 = bf16[384,768]{1,0:T(8,128)(2,1)S(1)} collective-permute-done((bf16[384,768]{1,0:T(8,128)(2,1)}, bf16[384,768]{1,0:T(8,128)(2,1)S(1)}, u32[]{:S(2)}, u32[]{:S(2)}) %collective-permute-start.11) | collective-permute-done | bytes 589856 | tf_op jit(solution)/shard_map/ppermute | solution.py:28
  335.6 11.1 collective-permute-done.5
  353.3 18.7 collective-permute-done.12
  372.9 14.0 collective-permute-done.6
  390.5 14.8 all_gather.49
  433.7 11.3 all_gather.56
  465.1 41.6 %all-gather.27.cloned.1.call-done = bf16[1,768,3072]{2,1,0:T(8,128)(2,1)} async-done(((bf16[1,96,3072]{2,1,0:T(8,128)(2,1)}), bf16[1,768,3072]{2,1,0:T(8,128)(2,1)}) %all-gather.27.cloned.1.call-update) | async-done | bytes 4718608 | tf_op jit(solution)/shard_map/all_gather | solution.py:119
  529.9 15.8 reduce-scatter.27.cloned.1.call-done
  583.5 15.6 reduce-scatter.31.cloned.1.call-done
  648.3 24.6 %reduce-scatter.39.cloned.1.call-done = f32[96,768]{1,0:T(8,128)} async-done(((f32[768,768]{1,0:T(8,128)}), f32[96,768]{1,0:T(8,128)}) %reduce-scatter.39.cloned.1.call-update) | async-done | bytes 294928 | tf_op jit(solution)/shard_map/reduce_scatter | solution.py:129
  672.9 72.8 %reduce-scatter.37.cloned.1.call-done = f32[96,768]{1,0:T(8,128)} async-done(((f32[768,768]{1,0:T(8,128)}), f32[96,768]{1,0:T(8,128)}) %reduce-scatter.37.cloned.1.call-update) | async-done | bytes 294928 | tf_op jit(solution)/shard_map/reduce_scatter | solution.py:129
  745.8 132.1 %reduce-scatter.35.cloned.1.call-done = f32[96,2304]{1,0:T(8,128)} async-done(((f32[768,2304]{1,0:T(8,128)}), f32[96,2304]{1,0:T(8,128)}) %reduce-scatter.35.cloned.1.call-update) | async-done | bytes 884752 | tf_op jit(solution)/shard_map/reduce_scatter | solution.py:128
  877.8 131.9 %reduce-scatter.33.cloned.1.call-done = f32[96,2304]{1,0:T(8,128)} async-done(((f32[768,2304]{1,0:T(8,128)}), f32[96,2304]{1,0:T(8,128)}) %reduce-scatter.33.cloned.1.call-update) | async-done | bytes 884752 | tf_op jit(solution)/shard_map/reduce_scatter | solution.py:128
  1009.7 164.7 %reduce-scatter.43.cloned.1.call-done = f32[96,3072]{1,0:T(8,128)} async-done(((f32[768,3072]{1,0:T(8,128)}), f32[96,3072]{1,0:T(8,128)}) %reduce-scatter.43.cloned.1.call-update) | async-done | bytes 1179664 | tf_op jit(solution)/shard_map/reduce_scatter | solution.py:130
  1174.4 164.7 %reduce-scatter.47.cloned.1.call-done = f32[384,768]{1,0:T(8,128)} async-done(((f32[3072,768]{1,0:T(8,128)}), f32[384,768]{1,0:T(8,128)}) %reduce-scatter.47.cloned.1.call-update) | async-done | bytes 1179664 | tf_op jit(solution)/shard_map/reduce_scatter | solution.py:131
  1339.1 164.7 %reduce-scatter.41.cloned.1.call-done = f32[96,3072]{1,0:T(8,128)} async-done(((f32[768,3072]{1,0:T(8,128)}), f32[96,3072]{1,0:T(8,128)}) %reduce-scatter.41.cloned.1.call-update) | async-done | bytes 1179664 | tf_op jit(solution)/shard_map/reduce_scatter | solution.py:130
  1503.8 164.7 %reduce-scatter.45.cloned.1.call-done = f32[384,768]{1,0:T(8,128)} async-done(((f32[3072,768]{1,0:T(8,128)}), f32[384,768]{1,0:T(8,128)}) %reduce-scatter.45.cloned.1.call-update) | async-done | bytes 1179664 | tf_op jit(solution)/shard_map/reduce_scatter | solution.py:131
  1674.3 59.3 %reduce-scatter.51.cloned.1.call-done = f32[96,2]{1,0:T(8,128)} async-done(((f32[768,2]{1,0:T(8,128)}), f32[96,2]{1,0:T(8,128)}) %reduce-scatter.51.cloned.1.call-update) | async-done | bytes 784
  1734.4 64.1 %reduce-scatter.55.cloned.1.call-done = f32[96,11]{1,0:T(8,128)} async-done(((f32[768,11]{1,0:T(8,128)}), f32[96,11]{1,0:T(8,128)}) %reduce-scatter.55.cloned.1.call-update) | async-done | bytes 4240
  1800.5 63.1 %reduce-scatter.49.cloned.1.call-done = f32[96,2]{1,0:T(8,128)} async-done(((f32[768,2]{1,0:T(8,128)}), f32[96,2]{1,0:T(8,128)}) %reduce-scatter.49.cloned.1.call-update) | async-done | bytes 784
  1864.4 64.1 %reduce-scatter.53.cloned.1.call-done = f32[96,11]{1,0:T(8,128)} async-done(((f32[768,11]{1,0:T(8,128)}), f32[96,11]{1,0:T(8,128)}) %reduce-scatter.53.cloned.1.call-update) | async-done | bytes 4240
  1929.4 11.1 all-reduce
  1943.6 119.4 %all-reduce.4.cloned.1.call-done = (f32[1,96,2304]{2,1,0:T(8,128)}, f32[1,96,2304]{2,1,0:T(8,128)}, f32[1,96,768]{2,1,0:T(8,128)}, f32[1,96,768]{2,1,0:T(8,128)}...) async-done(((f32[1,96,2304]{2,1,0:T(8,128)}, f32[1,96,2304]{2,1,0:T(8,128)}, f32[1,96,768]{2,1,0:T(8,128)}, ...) | async-done | bytes 7077904 | tf_op jit(solution)/shard_map/psum | solution.py:135
  (554 shorter events, 267.2 us)
Async XLA Ops:
  7.2 325.7 %all-gather.25.cloned.1.call-start = ((), (), s32[]{:S(2)}) async-start(), calls=%async_computation.32 | async-start | bytes 1327104 | tf_op jit(solution)/shard_map/all_gather | solution.py:118
  9.1 378.7 %all-gather.17.cloned.1.call-start = ((), (), s32[]{:S(2)}) async-start(), calls=%async_computation.28 | async-start | bytes 3981312 | tf_op jit(solution)/shard_map/all_gather | solution.py:117
  11.7 406.4 %all-gather.19.cloned.1.call-start = ((), (), s32[]{:S(2)}) async-start(), calls=%async_computation.29 | async-start | bytes 1327104 | tf_op jit(solution)/shard_map/all_gather | solution.py:118
  12.5 407.4 %all-gather.21.cloned.1.call-start = ((), (), s32[]{:S(2)}) async-start(), calls=%async_computation.30 | async-start | bytes 5308416 | tf_op jit(solution)/shard_map/all_gather | solution.py:119
  14.0 412.8 %all-gather.23.cloned.1.call-start = ((), (), s32[]{:S(2)}) async-start(), calls=%async_computation.31 | async-start | bytes 3981312 | tf_op jit(solution)/shard_map/all_gather | solution.py:117
  14.6 492.1 %all-gather.27.cloned.1.call-start = ((), (), s32[]{:S(2)}) async-start(), calls=%async_computation.33 | async-start | bytes 5308416 | tf_op jit(solution)/shard_map/all_gather | solution.py:119
  17.5 129.5 %collective-permute-start = (bf16[384,768]{1,0:T(8,128)(2,1)}, bf16[384,768]{1,0:T(8,128)(2,1)}, u32[]{:S(2)}, u32[]{:S(2)}) collective-permute-start(bf16[384,768]{1,0:T(8,128)(2,1)} %get-tuple-element.174), channel_id=1, source_target_pairs={{0,1},{1,2},{2,3},{3,4},{4,5},{5,6},{6,7},{7,0},{8,9},{9,10},{10,1... | collective-permute-start | bytes 1769480 | tf_op jit(solution)/shard_map/ppermute | solution.py:28
  20.5 130.9 %collective-permute-start.7 = (bf16[384,768]{1,0:T(8,128)(2,1)}, bf16[384,768]{1,0:T(8,128)(2,1)}, u32[]{:S(2)}, u32[]{:S(2)}) collective-permute-start(bf16[384,768]{1,0:T(8,128)(2,1)} %get-tuple-element.173), channel_id=1, source_target_pairs={{0,1},{1,2},{2,3},{3,4},{4,5},{5,6},{6,7},{7,0},{8,9},{9,10},{10,1... | collective-permute-start | bytes 1769480 | tf_op jit(solution)/shard_map/ppermute | solution.py:28
  22.0 503.3 %reduce-scatter.25.cloned.1.call-start = ((), (), s32[]{:S(2)}) async-start(), calls=%async_computation.16 | async-start | bytes 1179648 | tf_op jit(solution)/shard_map/reduce_scatter | solution.py:259
  169.6 36.0 %collective-permute-start.2 = (bf16[384,768]{1,0:T(8,128)(2,1)S(1)}, bf16[384,768]{1,0:T(8,128)(2,1)S(1)}, u32[]{:S(2)}, u32[]{:S(2)}) collective-permute-start(bf16[384,768]{1,0:T(8,128)(2,1)S(1)} %collective-permute-done.1), channel_id=1, source_target_pairs={{0,1},{1,2},{2,3},{3,4},{4,5},{5,6},{6,7},{7,0},{8,9},{9,10},{10,1... | collective-permute-start | bytes 1769480 | tf_op jit(solution)/shard_map/ppermute | solution.py:28
  221.9 83.2 %collective-permute-start.10 = (bf16[384,768]{1,0:T(8,128)(2,1)}, bf16[384,768]{1,0:T(8,128)(2,1)}, u32[]{:S(2)}, u32[]{:S(2)}) collective-permute-start(bf16[384,768]{1,0:T(8,128)(2,1)} %collective-permute-done.9), channel_id=1, source_target_pairs={{0,1},{1,2},{2,3},{3,4},{4,5},{5,6},{6,7},{7,0},{8,9},{9,10},{10,1... | collective-permute-start | bytes 1769480 | tf_op jit(solution)/shard_map/ppermute | solution.py:28
  240.6 67.4 %collective-permute-start.4 = (bf16[384,768]{1,0:T(8,128)(2,1)}, bf16[384,768]{1,0:T(8,128)(2,1)}, u32[]{:S(2)}, u32[]{:S(2)}) collective-permute-start(bf16[384,768]{1,0:T(8,128)(2,1)} %collective-permute-done.3), channel_id=1, source_target_pairs={{0,1},{1,2},{2,3},{3,4},{4,5},{5,6},{6,7},{7,0},{8,9},{9,10},{10,1... | collective-permute-start | bytes 1769480 | tf_op jit(solution)/shard_map/ppermute | solution.py:28
  308.0 38.7 %collective-permute-start.5 = (bf16[384,768]{1,0:T(8,128)(2,1)}, bf16[384,768]{1,0:T(8,128)(2,1)S(1)}, u32[]{:S(2)}, u32[]{:S(2)}) collective-permute-start(bf16[384,768]{1,0:T(8,128)(2,1)} %collective-permute-done.4), channel_id=1, source_target_pairs={{0,1},{1,2},{2,3},{3,4},{4,5},{5,6},{6,7},{7,0},{8,9},{9,10},{10,1... | collective-permute-start | bytes 1769480 | tf_op jit(solution)/shard_map/ppermute | solution.py:28
  332.9 39.1 %collective-permute-start.12 = (bf16[384,768]{1,0:T(8,128)(2,1)S(1)}, bf16[384,768]{1,0:T(8,128)(2,1)}, u32[]{:S(2)}, u32[]{:S(2)}) collective-permute-start(bf16[384,768]{1,0:T(8,128)(2,1)S(1)} %collective-permute-done.11), channel_id=1, source_target_pairs={{0,1},{1,2},{2,3},{3,4},{4,5},{5,6},{6,7},{7,0},{8,9},{9,10},{10,1... | collective-permute-start | bytes 1769480 | tf_op jit(solution)/shard_map/ppermute | solution.py:28
  346.7 40.3 %collective-permute-start.6 = (bf16[384,768]{1,0:T(8,128)(2,1)S(1)}, bf16[384,768]{1,0:T(8,128)(2,1)S(1)}, u32[]{:S(2)}, u32[]{:S(2)}) collective-permute-start(bf16[384,768]{1,0:T(8,128)(2,1)S(1)} %collective-permute-done.5), channel_id=1, source_target_pairs={{0,1},{1,2},{2,3},{3,4},{4,5},{5,6},{6,7},{7,0},{8,9},{9,10},{10,1... | collective-permute-start | bytes 1769480 | tf_op jit(solution)/shard_map/ppermute | solution.py:28
  372.0 89.1 %collective-permute-start.13 = (bf16[384,768]{1,0:T(8,128)(2,1)}, bf16[384,768]{1,0:T(8,128)(2,1)}, u32[]{:S(2)}, u32[]{:S(2)}) collective-permute-start(bf16[384,768]{1,0:T(8,128)(2,1)} %collective-permute-done.12), channel_id=1, source_target_pairs={{0,1},{1,2},{2,3},{3,4},{4,5},{5,6},{6,7},{7,0},{8,9},{9,10},{10,1... | collective-permute-start | bytes 1769480 | tf_op jit(solution)/shard_map/ppermute | solution.py:28
  459.1 86.6 %reduce-scatter.27.cloned.1.call-start = ((), (), s32[]{:S(2)}) async-start(), calls=%async_computation.17 | async-start | bytes 1179648 | tf_op jit(solution)/shard_map/reduce_scatter | solution.py:260
  515.5 63.4 %reduce-scatter.29.cloned.1.call-start = ((), (), s32[]{:S(2)}) async-start(), calls=%async_computation.18 | async-start | bytes 1179648 | tf_op jit(solution)/shard_map/reduce_scatter | solution.py:259
  561.3 37.9 %reduce-scatter.31.cloned.1.call-start = ((), (), s32[]{:S(2)}) async-start(), calls=%async_computation.19 | async-start | bytes 1179648 | tf_op jit(solution)/shard_map/reduce_scatter | solution.py:260
  564.1 108.8 %reduce-scatter.39.cloned.1.call-start = ((), (), s32[]{:S(2)}) async-start(), calls=%async_computation.23 | async-start | bytes 2654208 | tf_op jit(solution)/shard_map/reduce_scatter | solution.py:129
  567.1 178.7 %reduce-scatter.37.cloned.1.call-start = ((), (), s32[]{:S(2)}) async-start(), calls=%async_computation.22 | async-start | bytes 2654208 | tf_op jit(solution)/shard_map/reduce_scatter | solution.py:129
  570.0 307.8 %reduce-scatter.35.cloned.1.call-start = ((), (), s32[]{:S(2)}) async-start(), calls=%async_computation.21 | async-start | bytes 7962624 | tf_op jit(solution)/shard_map/reduce_scatter | solution.py:128
  575.4 434.2 %reduce-scatter.33.cloned.1.call-start = ((), (), s32[]{:S(2)}) async-start(), calls=%async_computation.20 | async-start | bytes 7962624 | tf_op jit(solution)/shard_map/reduce_scatter | solution.py:128
  604.6 569.8 %reduce-scatter.43.cloned.1.call-start = ((), (), s32[]{:S(2)}) async-start(), calls=%async_computation.25 | async-start | bytes 10616832 | tf_op jit(solution)/shard_map/reduce_scatter | solution.py:130
  611.6 727.4 %reduce-scatter.47.cloned.1.call-start = ((), (), s32[]{:S(2)}) async-start(), calls=%async_computation.27 | async-start | bytes 10616832 | tf_op jit(solution)/shard_map/reduce_scatter | solution.py:131
  617.7 886.1 %reduce-scatter.41.cloned.1.call-start = ((), (), s32[]{:S(2)}) async-start(), calls=%async_computation.24 | async-start | bytes 10616832 | tf_op jit(solution)/shard_map/reduce_scatter | solution.py:130
  628.8 1039.6 %reduce-scatter.45.cloned.1.call-start = ((), (), s32[]{:S(2)}) async-start(), calls=%async_computation.26 | async-start | bytes 10616832 | tf_op jit(solution)/shard_map/reduce_scatter | solution.py:131
  635.0 1098.5 %reduce-scatter.51.cloned.1.call-start = ((), (), s32[]{:S(2)}) async-start(), calls=%async_computation.35 | async-start | bytes 442368
  636.7 1161.8 %reduce-scatter.55.cloned.1.call-start = ((), (), s32[]{:S(2)}) async-start(), calls=%async_computation.37 | async-start | bytes 442368
  638.4 1225.1 %reduce-scatter.49.cloned.1.call-start = ((), (), s32[]{:S(2)}) async-start(), calls=%async_computation.34 | async-start | bytes 442368
  646.7 1281.9 %reduce-scatter.53.cloned.1.call-start = ((), (), s32[]{:S(2)}) async-start(), calls=%async_computation.36 | async-start | bytes 442368
  648.3 1414.7 %all-reduce.4.cloned.1.call-start = ((), (), s32[]{:S(2)}) async-start(), calls=%async_computation.38 | async-start | bytes 14155776 | tf_op jit(solution)/shard_map/psum | solution.py:135
  (143 other events, 4609.0 us)
Sparse Core Ops, SparseCore 0:
  10.8 65.1 all-gather.24
  78.7 77.5 all-gather.16
  159.1 51.5 all-gather.18
  213.3 107.7 all-gather.20
  323.7 102.1 all-gather.22
  428.6 78.0 all-gather.26
  509.5 15.8 reduce-scatter.24
  528.2 17.4 reduce-scatter.26
  561.4 17.4 reduce-scatter.28
  581.6 17.4 reduce-scatter.30
  603.2 69.6 reduce-scatter.38
  676.9 68.8 reduce-scatter.36
  749.4 128.3 reduce-scatter.34
  881.3 128.2 reduce-scatter.32
  1013.1 161.2 reduce-scatter.42
  1177.8 161.1 reduce-scatter.46
  1342.5 161.2 reduce-scatter.40
  1507.2 161.1 reduce-scatter.44
  1672.3 61.2 reduce-scatter.50
  1737.2 61.1 reduce-scatter.54
  1802.3 61.1 reduce-scatter.48
  1867.4 61.1 reduce-scatter.52
  1931.4 131.5 all-reduce.3
